TPU v7x, 128 devices: a whole 4x4x4 slice. The times are simulated.
128 devices in a mesh: row: 8 (over z, core), col: 16 (over x, y).
Axes of the slice: x: 4, y: 4, z: 4, core: 2. Of those that a mesh axis runs over, the one named last changes fastest.
Arguments:
- far_field: float32 [16384, 16384], P('row', 'col'), may hold values from -4 to 4, as said below
- inverses: float32 [2, 256, 256], replicated, may hold values from -0.05 to 0.06, as said below
- test_table: float32 [524288, 128], P(('row', 'col')), may hold values from -1.5 to 1.5
- trial_table: float32 [524288, 128], P(('row', 'col')), may hold values from -1.5 to 1.5
- tile_list: int32 [2048, 2], P(('row', 'col')), may hold values from 0 to 127, as said below
- tile_nodes: int32 [2048, 256], P(('row', 'col')), may hold values from 0 to 4095
- strokes: float32 [16384, 256], P('col'), may hold values from -0.046875 to 0.046875
Outputs:
- factored: float32 [16384, 16384], P('row', 'col')
- stroke_image: float32 [16384, 256], P('row')
Inputs may be any that keep to these rules, and one draw needn't show every extreme that they name: `tile_list`: tile t lies in the block rows held by the grid row of its pair owner (owners in row-major order of the device grid). At most 2 tiles of one owner fall in the block columns of one grid column, and in every grid row some grid column receives exactly 2 tiles from every owner of that row. Duplicate blocks may occur. `tile_nodes`: node indices refer to the owner's own 4096 table rows. `far_field`: entries of order one with a dominant diagonal between 2 and 4. `inverses`: each inverse has a positive diagonal and full off-diagonal entries.
All inputs are finite; a program needn't handle non-finite values.
Results may differ from a plain program's by a relative error of at most 0.0001.
Values sent between devices are 32-bit elements; how exact they have to be, the bound alone decides.
A program may use at most 128 MiB of HBM per device.

v0:
```python
import jax
import jax.numpy as jnp
from jax import lax
from jax.sharding import PartitionSpec as P


def broadcast(value, axis, source):
    kept = jnp.where(lax.axis_index(axis) == source, value, 0).astype(value.dtype)
    return lax.psum(kept, axis)


def rows_share(block):
    return broadcast(block, "row", 0)


def on_device(far_field, inverses, test_table, trial_table, tile_list, tile_nodes, strokes):
    highest = lax.Precision.HIGHEST
    col_count = lax.axis_size("col")
    row_index = lax.axis_index("row")
    col_index = lax.axis_index("col")
    rows_local, cols_local = far_field.shape
    tile = test_table.shape[1]
    width = inverses.shape[1]
    owned = tile_list.shape[0]
    capacity = 2 * ((owned + col_count - 1) // col_count)
    block_rows = rows_local // tile
    block_cols = cols_local // tile
    left = test_table[tile_nodes]
    right = trial_table[tile_nodes]
    pieces = jnp.einsum(
        "tqi,tqj->tij", left, right, precision=highest, preferred_element_type=jnp.float32
    )
    pieces = pieces.reshape(owned, tile * tile)
    target = tile_list[:, 1] // block_cols
    position = jnp.arange(owned, dtype=jnp.int32)
    earlier = (target[None, :] == target[:, None]) & (position[None, :] < position[:, None])
    slot = target * capacity + jnp.sum(earlier.astype(jnp.int32), axis=1)
    picked = jnp.arange(col_count * capacity, dtype=jnp.int32)[:, None] == slot[None, :]
    local_block = (tile_list[:, 0] - row_index * block_rows) * block_cols + tile_list[
        :, 1
    ] % block_cols
    outgoing = jnp.dot(
        picked.astype(jnp.float32), pieces, precision=highest, preferred_element_type=jnp.float32
    )
    outgoing = outgoing.reshape(col_count, capacity, tile * tile)
    labels = jnp.sum(jnp.where(picked, local_block[None, :] + 1, 0), axis=1) - 1
    labels = labels.reshape(col_count, capacity)
    arrived, spots = (
        lax.all_to_all(outgoing, "col", split_axis=0, concat_axis=0, tiled=True),
        lax.all_to_all(labels, "col", split_axis=0, concat_axis=0, tiled=True),
    )
    arrived = arrived.reshape(col_count * capacity, tile * tile)
    spots = spots.reshape(col_count * capacity)
    placing = (
        jnp.arange(block_rows * block_cols, dtype=jnp.int32)[:, None] == spots[None, :]
    ).astype(jnp.float32)
    near = jnp.dot(placing, arrived, precision=highest, preferred_element_type=jnp.float32)
    near = (
        near.reshape(block_rows, block_cols, tile, tile)
        .transpose(0, 2, 1, 3)
        .reshape(rows_local, cols_local)
    )
    matrix = far_field + near
    global_rows = row_index * rows_local + jnp.arange(rows_local, dtype=jnp.int32)
    global_cols = col_index * cols_local + jnp.arange(cols_local, dtype=jnp.int32)
    first_grid_col = col_index == 0
    for panel in range(2):
        low = panel * width
        high = low + width
        lower = jnp.dot(
            matrix[:, low:high],
            inverses[panel],
            precision=highest,
            preferred_element_type=jnp.float32,
        )
        lower = jnp.where(global_rows[:, None] >= high, lower, 0.0)
        lower_all = broadcast(lower, "col", 0)
        upper = jnp.where(global_cols[None, :] >= high, matrix[low:high, :], 0.0)
        upper_all = rows_share(upper)
        matrix = matrix - jnp.dot(
            lower_all, upper_all, precision=highest, preferred_element_type=jnp.float32
        )
        renewed = jnp.where(global_rows[:, None] >= high, lower_all, matrix[:, low:high])
        matrix = matrix.at[:, low:high].set(jnp.where(first_grid_col, renewed, matrix[:, low:high]))
    partial_image = jnp.dot(matrix, strokes, precision=highest, preferred_element_type=jnp.float32)
    image = lax.psum(partial_image, "col")
    return (matrix, image)


def solution(mesh):
    return jax.shard_map(
        on_device,
        mesh=mesh,
        in_specs=(
            P("row", "col"),
            P(),
            P(("row", "col"), None),
            P(("row", "col"), None),
            P(("row", "col"), None),
            P(("row", "col"), None),
            P("col", None),
        ),
        out_specs=(P("row", "col"), P("row", None)),
        check_vma=False,
    )
```

profile of v0, /device:TPU:0, one launch (start us, length us, event | category | flops | bytes accessed | tf_op | source)
XLA Modules:
  0.0 573.1 jit_solution(1673368568827543794)
XLA Ops:
  7.2 0.0 copy-start
  7.2 0.8 fusion.29
  8.0 0.8 fusion.30
  8.8 0.2 convert_reduce_fusion
  9.0 0.1 select_reduce_fusion
  9.1 0.7 sub.34
  9.8 7.1 %all-to-all-start = ((s32[16,1,2]{2,1,0:T(1,128)}), s32[16,1,2]{2,1,0:T(1,128)S(1)}, u32[]{:S(2)}, u32[]{:S(2)}) async-start(s32[16,1,2]{2,1,0:T(1,128)} %bitcast.3), calls=%async_computation | async-start | bytes 16384 | tf_op jit(solution)/shard_map/all_to_all | solution.py:50
  16.9 0.7 fusion.18
  17.7 0.0 copy-done
  17.7 14.2 %gather_fusion = f32[4096,128]{1,0:T(8,128)} fusion(f32[4096,128]{1,0:T(8,128)S(1)} %copy-done, s32[4096]{0:T(1024)S(1)} %broadcast_clamp_fusion), kind=kCustom, calls=%fused_computation | custom fusion | bytes 4210688 | tf_op jit(solution)/shard_map/gather | solution.py:28
  31.9 0.0 copy-start.6
  31.9 15.9 %gather_fusion.1 = f32[4096,128]{1,0:T(8,128)} fusion(f32[4096,128]{1,0:T(8,128)} %param.14, s32[4096]{0:T(1024)S(1)} %broadcast_clamp_fusion), kind=kCustom, calls=%fused_computation.1 | custom fusion | bytes 4210688 | tf_op jit(solution)/shard_map/gather | solution.py:29
  47.8 0.0 copy-done.6
  47.8 5.1 fusion.31
  52.9 1.2 reshape.237
  54.1 2.2 fusion.19
  56.3 2.9 copy.19
  59.3 0.0 all-to-all-done
  59.3 7.2 %all-to-all-start.1 = ((f32[16,2,16384]{2,1,0:T(2,128)}), f32[16,2,16384]{2,1,0:T(2,128)S(1)}, u32[]{:S(2)}, u32[]{:S(2)}) async-start(f32[16,2,16384]{2,1,0:T(2,128)} %copy.19), calls=%async_computation.1 | async-start | bytes 4194304 | tf_op jit(solution)/shard_map/all_to_all | solution.py:49
  66.5 0.2 all-reduce.8.cloned.1.call-start
  66.8 0.5 broadcast.303
  67.3 0.7 reduce.19
  67.9 0.1 eq.93
  68.0 27.8 %all-to-all-done.1 = f32[16,2,16384]{2,1,0:T(2,128)S(1)} async-done(((f32[16,2,16384]{2,1,0:T(2,128)}), f32[16,2,16384]{2,1,0:T(2,128)S(1)}, u32[]{:S(2)}, u32[]{:S(2)}) %all-to-all-start.1) | async-done | bytes 2097184 | tf_op jit(solution)/shard_map/all_to_all | solution.py:49
  95.8 2.4 reshape.215
  98.2 7.3 %fusion.4 = f32[16,8,128,128]{3,1,2,0:T(8,128)} fusion(s32[32]{0:T(128)S(1)} %eq.93, s32[16,8]{1,0:T(8,128)S(1)} %multiply_add_fusion, f32[32,16384]{1,0:T(8,128)} %reshape.215), kind=kOutput, calls=%fused_computation.14 | convolution fusion | flops 805310464 | bytes 10486400 | tf_op jit(solution)/shard_map/dot_general | solution.py:57
  105.6 12.1 %bitcast_add_fusion = f32[2048,1024]{1,0:T(8,128)} fusion(f32[2048,1024]{1,0:T(8,128)} %param.11, f32[256,8,8,128]{3,2,1,0:T(8,128)} %bitcast.63), kind=kLoop, calls=%fused_computation.2 | loop fusion | flops 2097152 | bytes 25165824 | tf_op jit(solution)/shard_map/add | solution.py:63
  117.7 2.4 fusion.9
  120.1 0.0 all-reduce.8.cloned.1.call-update
  120.1 0.0 all-reduce.6.cloned.1.call-start
  120.2 0.0 copy-done.8
  120.2 4.7 fusion.1
  124.9 0.0 all-reduce.6.cloned.1.call-update
  125.0 0.3 all-reduce.12.cloned.1.call-start
  125.2 0.7 compare_reduce_fusion.1
  125.9 56.5 %all-reduce.8.cloned.1.call-done = f32[256,1024]{1,0:T(8,128)} async-done(((f32[256,1024]{1,0:T(8,128)}), f32[256,1024]{1,0:T(8,128)}) %all-reduce.8.cloned.1.call-update) | async-done | bytes 1048592 | tf_op jit(solution)/shard_map/psum | solution.py:9
  182.4 94.0 %all-reduce.6.cloned.1.call-done = f32[2048,256]{1,0:T(8,128)} async-done(((f32[2048,256]{1,0:T(8,128)}), f32[2048,256]{1,0:T(8,128)}) %all-reduce.6.cloned.1.call-update) | async-done | bytes 2097168 | tf_op jit(solution)/shard_map/psum | solution.py:9
  276.5 10.6 %convolution_subtract_fusion.1 = f32[2048,1024]{1,0:T(8,128)S(1)} fusion(f32[2048,1024]{1,0:T(8,128)} %bitcast_add_fusion, f32[2048,256]{1,0:T(8,128)} %all-reduce.6.cloned.1.call-done, f32[256,1024]{1,0:T(8,128)} %all-reduce.8.cloned.1.call-done), kind=kOutput, calls=%fused_computation.4 | convolution fusion | flops 6444548096 | bytes 19922944 | tf_op jit(solution)/shard_map/dot_general | solution.py:80
  287.0 0.0 copy-done.4
  287.0 1.2 fusion.2
  288.3 0.0 copy-start.3
  288.3 3.4 copy-done.3
  291.7 1.1 fusion.8
  292.8 0.0 all-reduce.12.cloned.1.call-update
  292.9 0.0 all-reduce.10.cloned.1.call-start
  292.9 4.7 fusion
  297.7 0.0 all-reduce.10.cloned.1.call-update
  297.7 0.3 all-reduce.14.cloned.1.call-start
  298.0 0.6 compare_reduce_fusion
  298.6 56.8 %all-reduce.12.cloned.1.call-done = f32[256,1024]{1,0:T(8,128)} async-done(((f32[256,1024]{1,0:T(8,128)}), f32[256,1024]{1,0:T(8,128)}) %all-reduce.12.cloned.1.call-update) | async-done | bytes 1048592 | tf_op jit(solution)/shard_map/psum | solution.py:9
  355.4 93.8 %all-reduce.10.cloned.1.call-done = f32[2048,256]{1,0:T(8,128)} async-done(((f32[2048,256]{1,0:T(8,128)}), f32[2048,256]{1,0:T(8,128)}) %all-reduce.10.cloned.1.call-update) | async-done | bytes 2097168 | tf_op jit(solution)/shard_map/psum | solution.py:9
  449.3 10.6 %convolution_subtract_fusion = f32[2048,1024]{1,0:T(8,128)S(1)} fusion(f32[2048,1024]{1,0:T(8,128)} %copy-done.3, f32[2048,256]{1,0:T(8,128)} %all-reduce.10.cloned.1.call-done, f32[256,1024]{1,0:T(8,128)} %all-reduce.12.cloned.1.call-done), kind=kOutput, calls=%fused_computation.3 | convolution fusion | flops 6444548096 | bytes 19922944 | tf_op jit(solution)/shard_map/dot_general | solution.py:80
  459.9 0.0 copy-done.5
  459.9 0.0 copy-start.7
  459.9 1.4 fusion.3
  461.2 0.0 copy-start.2
  461.3 3.4 copy-done.2
  464.6 0.0 copy-done.7
  464.7 8.3 %fusion.32 = f32[2048,256]{1,0:T(8,128)} fusion(f32[2048,1024]{1,0:T(8,128)S(1)} %fusion.3, f32[1024,256]{1,0:T(8,128)S(1)} %copy-done.7), kind=kOutput, calls=%fused_computation.69 | convolution fusion | flops 6442450944 | bytes 11534336 | tf_op jit(solution)/shard_map/dot_general | solution.py:85
  472.9 0.0 all-reduce.14.cloned.1.call-update
  472.9 0.0 copy-start.1
  473.0 90.5 %all-reduce.14.cloned.1.call-done = f32[2048,256]{1,0:T(8,128)} async-done(((f32[2048,256]{1,0:T(8,128)}), f32[2048,256]{1,0:T(8,128)}) %all-reduce.14.cloned.1.call-update) | async-done | bytes 2097168 | tf_op jit(solution)/shard_map/psum | solution.py:86
  563.5 3.0 copy.38
  566.5 0.0 copy-done.1
  (13 shorter events, 0.1 us)
Async XLA Ops:
  7.2 10.5 %copy-start = (f32[4096,128]{1,0:T(8,128)S(1)}, f32[4096,128]{1,0:T(8,128)}, u32[]{:S(2)}) copy-start(f32[4096,128]{1,0:T(8,128)} %param.13) | copy-start | bytes 6291460
  9.8 49.5 %all-to-all-start = ((s32[16,1,2]{2,1,0:T(1,128)}), s32[16,1,2]{2,1,0:T(1,128)S(1)}, u32[]{:S(2)}, u32[]{:S(2)}) async-start(s32[16,1,2]{2,1,0:T(1,128)} %bitcast.3), calls=%async_computation | async-start | bytes 16384 | tf_op jit(solution)/shard_map/all_to_all | solution.py:50
  31.9 15.9 %copy-start.6 = (f32[4096,128]{1,0:T(8,128)S(1)}, f32[4096,128]{1,0:T(8,128)}, u32[]{:S(2)}) copy-start(f32[4096,128]{1,0:T(8,128)} %gather_fusion) | copy-start | bytes 6291460
  59.3 36.5 %all-to-all-start.1 = ((f32[16,2,16384]{2,1,0:T(2,128)}), f32[16,2,16384]{2,1,0:T(2,128)S(1)}, u32[]{:S(2)}, u32[]{:S(2)}) async-start(f32[16,2,16384]{2,1,0:T(2,128)} %copy.19), calls=%async_computation.1 | async-start | bytes 4194304 | tf_op jit(solution)/shard_map/all_to_all | solution.py:49
  66.5 115.9 %all-reduce.8.cloned.1.call-start = ((), (), s32[]{:S(2)}) async-start(), calls=%async_computation.3 | async-start | bytes 2097152 | tf_op jit(solution)/shard_map/psum | solution.py:9
  117.7 2.5 copy-start.8
  120.1 156.3 %all-reduce.6.cloned.1.call-start = ((), (), s32[]{:S(2)}) async-start(), calls=%async_computation.2 | async-start | bytes 4194304 | tf_op jit(solution)/shard_map/psum | solution.py:9
  125.0 230.5 %all-reduce.12.cloned.1.call-start = ((), (), s32[]{:S(2)}) async-start(), calls=%async_computation.5 | async-start | bytes 2097152 | tf_op jit(solution)/shard_map/psum | solution.py:9
  276.5 10.6 %copy-start.4 = (f32[2048,256]{1,0:T(8,128)S(1)}, f32[2048,256]{1,0:T(8,128)}, u32[]{:S(2)}) copy-start(f32[2048,256]{1,0:T(8,128)} %all-reduce.6.cloned.1.call-done) | copy-start | bytes 6291460
  288.3 3.4 copy-start.3
  292.9 156.4 %all-reduce.10.cloned.1.call-start = ((), (), s32[]{:S(2)}) async-start(), calls=%async_computation.4 | async-start | bytes 4194304 | tf_op jit(solution)/shard_map/psum | solution.py:9
  297.7 265.8 %all-reduce.14.cloned.1.call-start = ((), (), s32[]{:S(2)}) async-start(), calls=%async_computation.6 | async-start | bytes 4194304 | tf_op jit(solution)/shard_map/psum | solution.py:86
  449.3 10.6 %copy-start.5 = (f32[2048,256]{1,0:T(8,128)S(1)}, f32[2048,256]{1,0:T(8,128)}, u32[]{:S(2)}) copy-start(f32[2048,256]{1,0:T(8,128)} %all-reduce.10.cloned.1.call-done) | copy-start | bytes 6291460
  459.9 4.8 copy-start.7
  461.2 3.4 copy-start.2
  472.9 93.6 %copy-start.1 = (f32[4096,128]{1,0:T(8,128)S(1)}, f32[4096,128]{1,0:T(8,128)}, u32[]{:S(2)}) copy-start(f32[4096,128]{1,0:T(8,128)} %param.13) | copy-start | bytes 6291460
Sparse Core Ops, SparseCore 0:
  120.3 62.1 all-reduce.7
  186.3 90.0 all-reduce.5
  293.0 62.3 all-reduce.11
  359.2 90.0 all-reduce.9
  473.1 90.3 all-reduce.13
where the time goes:
time: 574 us; the launch traced here: 573 us
  waiting for transfers between devices  420 us (73%)
  matrix products  53.5 us (9%)
  local copies, waits for them, and re-layouts  47.8 us (8%)
  other arithmetic  23 us (4%)
  starting transfers between devices  15.2 us (3%)
  between operations  14 us (2%)
    psum x4, waiting for transfers between devices, broadcast(): return lax.psum(kept, axis)  301 us
    psum x1, waiting for transfers between devices, on_device(): image = lax.psum(partial_image, 'col')  90.5 us
    all_to_all x1, waiting for transfers between devices, on_device(): lax.all_to_all(outgoing, 'col', split_axis=0, concat_axis=0, tiled=True)  27.8 us
    dot_general x2, matrix products, on_device(): jnp.dot(lower_all, upper_all, precision=highest, preferred_element_type=j...  21.1 us
    gather x1, local copies, waits for them, and re-layouts, on_device(): right = trial_table[tile_nodes]  15.9 us
    gather x1, local copies, waits for them, and re-layouts, on_device(): left = test_table[tile_nodes]  14.2 us
    add x1, other arithmetic, on_device(): matrix = far_field + near  12.1 us
  transfers between devices with their start and end apart: 7, of which 6 were waited for; matrix products, arithmetic and copies ran while one was open for 9% of the time, Pallas kernels for 0%

commit v1 on v0

--- a/solution.py
+++ b/solution.py
@@ -1,7 +1,16 @@
+import functools
 import jax
 import jax.numpy as jnp
 from jax import lax
 from jax.sharding import PartitionSpec as P
+
+
+def target_check(work_x, row_axis):
+    passed = lax.all_gather(work_x, row_axis).sum(axis=0)
+    return passed
+
+
+post_the_view = functools.partial(target_check, row_axis="col")
 
 
 def broadcast(value, axis, source):
@@ -83,7 +92,7 @@
         renewed = jnp.where(global_rows[:, None] >= high, lower_all, matrix[:, low:high])
         matrix = matrix.at[:, low:high].set(jnp.where(first_grid_col, renewed, matrix[:, low:high]))
     partial_image = jnp.dot(matrix, strokes, precision=highest, preferred_element_type=jnp.float32)
-    image = lax.psum(partial_image, "col")
+    image = post_the_view(partial_image)
     return (matrix, image)
 
 

time: 574 us -> 691 us (1.20)
  waiting for transfers between devices: 420 us -> 526 us
  other arithmetic: 23 us -> 36.4 us
    all_gather x0 -> x1, waiting for transfers between devices: none -> 197 us  [target_check(): passed = lax.all_gather(work_x, row_axis).sum(axis=0)]
    psum x1 -> x0, waiting for transfers between devices: 90.5 us -> none  [on_device(): image = lax.psum(partial_image, 'col')]
    reduce_sum x0 -> x1, other arithmetic: none -> 13.5 us  [target_check(): passed = lax.all_gather(work_x, row_axis).sum(axis=0)]
  transfers between devices with their start and end apart: 7 -> 7, of which waited for: 6 -> 6; matrix products, arithmetic and copies ran while one was open for 9% -> 8% of each run, Pallas kernels for 0% -> 0%
where the time goes in v1:
time: 691 us; the launch traced here: 689 us
  waiting for transfers between devices  526 us (76%)
  matrix products  53.5 us (8%)
  local copies, waits for them, and re-layouts  44.8 us (6%)
  other arithmetic  36.4 us (5%)
  starting transfers between devices  15.2 us (2%)
  between operations  14 us (2%)
    psum x4, waiting for transfers between devices, broadcast(): return lax.psum(kept, axis)  301 us
    all_gather x1, waiting for transfers between devices, target_check(): passed = lax.all_gather(work_x, row_axis).sum(axis=0)  197 us
    all_to_all x1, waiting for transfers between devices, on_device(): lax.all_to_all(outgoing, 'col', split_axis=0, concat_axis=0, tiled=True)  27.8 us
    dot_general x2, matrix products, on_device(): jnp.dot(lower_all, upper_all, precision=highest, preferred_element_type=j...  21.1 us
    gather x1, local copies, waits for them, and re-layouts, on_device(): left = test_table[tile_nodes]  15.9 us
    gather x1, local copies, waits for them, and re-layouts, on_device(): right = trial_table[tile_nodes]  14.2 us
  transfers between devices with their start and end apart: 7, of which 6 were waited for; matrix products, arithmetic and copies ran while one was open for 8% of the time, Pallas kernels for 0%

profile of v1, /device:TPU:0, one launch (start us, length us, event | category | flops | bytes accessed | tf_op | source)
XLA Modules:
  0.0 689.5 jit_solution(9226059793749268030)
XLA Ops:
  7.2 0.0 copy-start
  7.2 0.8 fusion.29
  8.0 0.8 fusion.30
  8.8 0.2 convert_reduce_fusion
  9.0 0.1 select_reduce_fusion
  9.1 0.7 sub.34
  9.8 7.1 %all-to-all-start = ((s32[16,1,2]{2,1,0:T(1,128)}), s32[16,1,2]{2,1,0:T(1,128)S(1)}, u32[]{:S(2)}, u32[]{:S(2)}) async-start(s32[16,1,2]{2,1,0:T(1,128)} %bitcast.3), calls=%async_computation | async-start | bytes 16384 | tf_op jit(solution)/shard_map/all_to_all | solution.py:59
  16.9 0.7 fusion.18
  17.7 0.0 copy-done
  17.7 14.2 %gather_fusion.1 = f32[4096,128]{1,0:T(8,128)} fusion(f32[4096,128]{1,0:T(8,128)S(1)} %copy-done, s32[4096]{0:T(1024)S(1)} %broadcast_clamp_fusion), kind=kCustom, calls=%fused_computation.1 | custom fusion | bytes 4210688 | tf_op jit(solution)/shard_map/gather | solution.py:38
  31.9 0.0 copy-start.6
  31.9 15.9 %gather_fusion = f32[4096,128]{1,0:T(8,128)} fusion(f32[4096,128]{1,0:T(8,128)} %param.13, s32[4096]{0:T(1024)S(1)} %broadcast_clamp_fusion), kind=kCustom, calls=%fused_computation | custom fusion | bytes 4210688 | tf_op jit(solution)/shard_map/gather | solution.py:37
  47.8 0.0 copy-done.6
  47.8 5.1 fusion.31
  52.9 1.2 reshape.238
  54.1 2.2 fusion.19
  56.3 2.9 copy.19
  59.3 0.0 all-to-all-done
  59.3 7.2 %all-to-all-start.1 = ((f32[16,2,16384]{2,1,0:T(2,128)}), f32[16,2,16384]{2,1,0:T(2,128)S(1)}, u32[]{:S(2)}, u32[]{:S(2)}) async-start(f32[16,2,16384]{2,1,0:T(2,128)} %copy.19), calls=%async_computation.1 | async-start | bytes 4194304 | tf_op jit(solution)/shard_map/all_to_all | solution.py:58
  66.5 0.2 all-reduce.7.cloned.1.call-start
  66.8 0.5 broadcast.303
  67.3 0.7 reduce.19
  67.9 0.1 eq.93
  68.0 27.8 %all-to-all-done.1 = f32[16,2,16384]{2,1,0:T(2,128)S(1)} async-done(((f32[16,2,16384]{2,1,0:T(2,128)}), f32[16,2,16384]{2,1,0:T(2,128)S(1)}, u32[]{:S(2)}, u32[]{:S(2)}) %all-to-all-start.1) | async-done | bytes 2097184 | tf_op jit(solution)/shard_map/all_to_all | solution.py:58
  95.8 2.4 reshape.215
  98.2 7.3 %fusion.4 = f32[16,8,128,128]{3,1,2,0:T(8,128)} fusion(s32[32]{0:T(128)S(1)} %eq.93, s32[16,8]{1,0:T(8,128)S(1)} %multiply_add_fusion, f32[32,16384]{1,0:T(8,128)} %reshape.215), kind=kOutput, calls=%fused_computation.14 | convolution fusion | flops 805310464 | bytes 10486400 | tf_op jit(solution)/shard_map/dot_general | solution.py:66
  105.6 12.1 %bitcast_add_fusion = f32[2048,1024]{1,0:T(8,128)} fusion(f32[2048,1024]{1,0:T(8,128)} %param.11, f32[256,8,8,128]{3,2,1,0:T(8,128)} %bitcast.64), kind=kLoop, calls=%fused_computation.2 | loop fusion | flops 2097152 | bytes 25165824 | tf_op jit(solution)/shard_map/add | solution.py:72
  117.7 0.0 copy-start.8
  117.7 2.4 fusion.9
  120.1 0.0 all-reduce.7.cloned.1.call-update
  120.1 0.0 all-reduce.5.cloned.1.call-start
  120.2 0.0 copy-done.8
  120.2 4.7 fusion.1
  124.9 0.0 all-reduce.5.cloned.1.call-update
  125.0 0.3 all-reduce.11.cloned.1.call-start
  125.2 0.7 compare_reduce_fusion.1
  125.9 56.5 %all-reduce.7.cloned.1.call-done = f32[256,1024]{1,0:T(8,128)} async-done(((f32[256,1024]{1,0:T(8,128)}), f32[256,1024]{1,0:T(8,128)}) %all-reduce.7.cloned.1.call-update) | async-done | bytes 1048592 | tf_op jit(solution)/shard_map/psum | solution.py:18
  182.4 94.0 %all-reduce.5.cloned.1.call-done = f32[2048,256]{1,0:T(8,128)} async-done(((f32[2048,256]{1,0:T(8,128)}), f32[2048,256]{1,0:T(8,128)}) %all-reduce.5.cloned.1.call-update) | async-done | bytes 2097168 | tf_op jit(solution)/shard_map/psum | solution.py:18
  276.5 10.6 %convolution_subtract_fusion.1 = f32[2048,1024]{1,0:T(8,128)S(1)} fusion(f32[2048,1024]{1,0:T(8,128)} %bitcast_add_fusion, f32[2048,256]{1,0:T(8,128)} %all-reduce.5.cloned.1.call-done, f32[256,1024]{1,0:T(8,128)} %all-reduce.7.cloned.1.call-done), kind=kOutput, calls=%fused_computation.4 | convolution fusion | flops 6444548096 | bytes 19922944 | tf_op jit(solution)/shard_map/dot_general | solution.py:89
  287.0 0.0 copy-done.4
  287.0 1.2 fusion.2
  288.3 0.0 copy-start.3
  288.3 3.4 copy-done.3
  291.7 1.1 fusion.8
  292.8 0.0 all-reduce.11.cloned.1.call-update
  292.9 0.0 all-reduce.9.cloned.1.call-start
  292.9 4.7 fusion
  297.7 0.0 all-reduce.9.cloned.1.call-update
  297.7 0.3 all-gather.3.cloned.1.call-start
  298.0 0.6 compare_reduce_fusion
  298.6 56.8 %all-reduce.11.cloned.1.call-done = f32[256,1024]{1,0:T(8,128)} async-done(((f32[256,1024]{1,0:T(8,128)}), f32[256,1024]{1,0:T(8,128)}) %all-reduce.11.cloned.1.call-update) | async-done | bytes 1048592 | tf_op jit(solution)/shard_map/psum | solution.py:18
  355.4 93.8 %all-reduce.9.cloned.1.call-done = f32[2048,256]{1,0:T(8,128)} async-done(((f32[2048,256]{1,0:T(8,128)}), f32[2048,256]{1,0:T(8,128)}) %all-reduce.9.cloned.1.call-update) | async-done | bytes 2097168 | tf_op jit(solution)/shard_map/psum | solution.py:18
  449.3 10.6 %convolution_subtract_fusion = f32[2048,1024]{1,0:T(8,128)S(1)} fusion(f32[2048,1024]{1,0:T(8,128)} %copy-done.3, f32[2048,256]{1,0:T(8,128)} %all-reduce.9.cloned.1.call-done, f32[256,1024]{1,0:T(8,128)} %all-reduce.11.cloned.1.call-done), kind=kOutput, calls=%fused_computation.3 | convolution fusion | flops 6444548096 | bytes 19922944 | tf_op jit(solution)/shard_map/dot_general | solution.py:89
  459.9 0.0 copy-done.5
  459.9 0.0 copy-start.7
  459.9 1.4 fusion.3
  461.2 0.0 copy-start.2
  461.3 3.4 copy-done.2
  464.6 0.0 copy-done.7
  464.7 8.3 %fusion.32 = f32[2048,256]{1,0:T(8,128)} fusion(f32[2048,1024]{1,0:T(8,128)S(1)} %fusion.3, f32[1024,256]{1,0:T(8,128)S(1)} %copy-done.7), kind=kOutput, calls=%fused_computation.69 | convolution fusion | flops 6442450944 | bytes 11534336 | tf_op jit(solution)/shard_map/dot_general | solution.py:94
  472.9 0.0 all-gather.3.cloned.1.call-update
  472.9 196.5 %all-gather.3.cloned.1.call-done = f32[32768,256]{1,0:T(8,128)} async-done(((f32[2048,256]{1,0:T(8,128)}), f32[32768,256]{1,0:T(8,128)}) %all-gather.3.cloned.1.call-update) | async-done | bytes 33554448 | tf_op jit(solution)/shard_map/all_gather | solution.py:9
  669.5 13.5 %reduce_sum.29 = f32[2048,256]{1,0:T(8,128)} reduce(f32[16,2048,256]{2,1,0:T(8,128)} %bitcast.65, f32[]{:T(128)} %constant.113.clone.1), dimensions={0}, to_apply=%region_8.9 | reduce | flops 7864320 | bytes 35651588 | tf_op jit(solution)/shard_map/reduce_sum | solution.py:9
  683.0 0.0 copy-done.1
  (13 shorter events, 0.1 us)
Async XLA Ops:
  7.2 10.5 %copy-start = (f32[4096,128]{1,0:T(8,128)S(1)}, f32[4096,128]{1,0:T(8,128)}, u32[]{:S(2)}) copy-start(f32[4096,128]{1,0:T(8,128)} %param.14) | copy-start | bytes 6291460
  9.8 49.5 %all-to-all-start = ((s32[16,1,2]{2,1,0:T(1,128)}), s32[16,1,2]{2,1,0:T(1,128)S(1)}, u32[]{:S(2)}, u32[]{:S(2)}) async-start(s32[16,1,2]{2,1,0:T(1,128)} %bitcast.3), calls=%async_computation | async-start | bytes 16384 | tf_op jit(solution)/shard_map/all_to_all | solution.py:59
  31.9 15.9 %copy-start.6 = (f32[4096,128]{1,0:T(8,128)S(1)}, f32[4096,128]{1,0:T(8,128)}, u32[]{:S(2)}) copy-start(f32[4096,128]{1,0:T(8,128)} %gather_fusion.1) | copy-start | bytes 6291460
  59.3 36.5 %all-to-all-start.1 = ((f32[16,2,16384]{2,1,0:T(2,128)}), f32[16,2,16384]{2,1,0:T(2,128)S(1)}, u32[]{:S(2)}, u32[]{:S(2)}) async-start(f32[16,2,16384]{2,1,0:T(2,128)} %copy.19), calls=%async_computation.1 | async-start | bytes 4194304 | tf_op jit(solution)/shard_map/all_to_all | solution.py:58
  66.5 115.9 %all-reduce.7.cloned.1.call-start = ((), (), s32[]{:S(2)}) async-start(), calls=%async_computation.3 | async-start | bytes 2097152 | tf_op jit(solution)/shard_map/psum | solution.py:18
  117.7 2.5 copy-start.8
  120.1 156.3 %all-reduce.5.cloned.1.call-start = ((), (), s32[]{:S(2)}) async-start(), calls=%async_computation.2 | async-start | bytes 4194304 | tf_op jit(solution)/shard_map/psum | solution.py:18
  125.0 230.5 %all-reduce.11.cloned.1.call-start = ((), (), s32[]{:S(2)}) async-start(), calls=%async_computation.5 | async-start | bytes 2097152 | tf_op jit(solution)/shard_map/psum | solution.py:18
  276.5 10.6 %copy-start.4 = (f32[2048,256]{1,0:T(8,128)S(1)}, f32[2048,256]{1,0:T(8,128)}, u32[]{:S(2)}) copy-start(f32[2048,256]{1,0:T(8,128)} %all-reduce.5.cloned.1.call-done) | copy-start | bytes 6291460
  288.3 3.4 copy-start.3
  292.9 156.4 %all-reduce.9.cloned.1.call-start = ((), (), s32[]{:S(2)}) async-start(), calls=%async_computation.4 | async-start | bytes 4194304 | tf_op jit(solution)/shard_map/psum | solution.py:18
  297.7 371.8 %all-gather.3.cloned.1.call-start = ((), (), s32[]{:S(2)}) async-start(), calls=%async_computation.6 | async-start | bytes 35651584 | tf_op jit(solution)/shard_map/all_gather | solution.py:9
  449.3 10.6 %copy-start.5 = (f32[2048,256]{1,0:T(8,128)S(1)}, f32[2048,256]{1,0:T(8,128)}, u32[]{:S(2)}) copy-start(f32[2048,256]{1,0:T(8,128)} %all-reduce.9.cloned.1.call-done) | copy-start | bytes 6291460
  459.9 4.8 copy-start.7
  461.2 3.4 copy-start.2
  669.5 13.5 %copy-start.1 = (f32[4096,128]{1,0:T(8,128)S(1)}, f32[4096,128]{1,0:T(8,128)}, u32[]{:S(2)}) copy-start(f32[4096,128]{1,0:T(8,128)} %param.14) | copy-start | bytes 6291460
Sparse Core Ops, SparseCore 0:
  120.3 62.1 all-reduce.6
  186.3 90.0 all-reduce.4
  293.0 62.3 all-reduce.10
  359.2 90.0 all-reduce.8
  473.1 196.3 all-gather.2
